TPU v7x, 512 devices: a whole 4x4x16 slice. The times are simulated.
512 devices in a mesh: ctx: 64 (over y, z), tp: 8 (over x, core).
Axes of the slice: x: 4, y: 4, z: 16, core: 2. Of those that a mesh axis runs over, the one named last changes fastest.
Arguments:
- gate_out: bfloat16 [32768, 4096], P('ctx', 'tp'), may hold values from -6 to 6
- gate_in: bfloat16 [32768, 4096], P('ctx', 'tp'), may hold values from -6 to 6
- signal: bfloat16 [32768, 4096], P('ctx', 'tp'), may hold values from -6 to 6
- decay_rates: float32 [16, 4096], P(None, 'tp'), may hold values from 9.765625e-07 to 0.1, as said below
- residues: float32 [16, 4096], P(None, 'tp'), may hold values from -0.6 to 0.6
- skip_gain: float32 [4096], P('tp'), may hold values from -4 to 4
- out_proj: bfloat16 [4096, 4096], P('tp'), may hold values from -0.09375 to 0.09375
- doc_lengths: int32 [32], replicated, may hold values from 1 to 20480, 32768 in all
Outputs:
- layer_out: bfloat16 [32768, 4096], P(('ctx', 'tp'))
Inputs may be any that keep to these rules, and one draw needn't show every extreme that they name: `doc_lengths`: 32 documents laid end to end, lengths summing to 32768. `decay_rates`: positive.
All inputs are finite; a program needn't handle non-finite values.
Results may differ from a plain program's by a relative error of at most 0.017.
Values may be sent and summed in bfloat16 or wider, within the bound.
No kernel may reach another device: no remote copies, remote signals or barrier semaphores. Data moves between devices by JAX's collectives and lax.ppermute only.
A program may use at most 64 MiB of HBM per device.

v0:
```python
import jax
import jax.numpy as jnp
from jax import lax
from jax.sharding import PartitionSpec as P

precise = lax.Precision.HIGHEST


def per_device(gate_out, gate_in, signal, decay_rates, residues, skip_gain, out_proj, doc_lengths):
    length = signal.shape[0]
    channels = signal.shape[1]
    block_len = min(32, length)
    num_blocks = length // block_len
    my_shard = lax.axis_index("ctx")
    shard_begin = my_shard * length
    doc_ends = jnp.cumsum(doc_lengths)
    doc_starts = doc_ends - doc_lengths
    positions = shard_begin + jnp.arange(length, dtype=jnp.int32)
    doc_index = jnp.sum((doc_starts[None, :] <= positions[:, None]).astype(jnp.int32), axis=1)
    opening = jnp.any(doc_starts[None, :] == positions[:, None], axis=1)
    head_start = jnp.max(jnp.where(doc_starts <= shard_begin, doc_starts, 0))
    open_shard = ((doc_index == doc_index[0]) & (head_start < shard_begin)).astype(jnp.float32)
    anchor = head_start // length
    feed_in = gate_in.astype(jnp.float32) * signal.astype(jnp.float32)
    lag_steps = jnp.arange(block_len, dtype=jnp.float32)
    lag_decay = jnp.exp(-lag_steps[None, :, None] * decay_rates[:, None, :])
    filter_taps = jnp.einsum("nkc,nc->kc", lag_decay, residues, precision=precise)
    lag_ids = jnp.arange(block_len, dtype=jnp.int32)
    onehot = (lag_ids[:, None, None] - lag_ids[None, :, None] == lag_ids[None, None, :]).astype(
        jnp.float32
    )
    toeplitz = jnp.einsum("tsk,kc->tsc", onehot, filter_taps, precision=precise)
    enter_decay = jnp.exp(-(lag_steps + 1.0)[None, :, None] * decay_rates[:, None, :])
    leave_decay = jnp.exp(-(block_len - 1.0 - lag_steps)[None, :, None] * decay_rates[:, None, :])
    block_decay = jnp.exp(-block_len * decay_rates)

    def advance(carry_state, inputs):
        block_rows, block_docs, block_marks = inputs
        same_doc = (block_docs[:, None] == block_docs[None, :]).astype(jnp.float32)
        within = jnp.einsum(
            "tsc,sc->tc", toeplitz * same_doc[:, :, None], block_rows, precision=precise
        )
        before = (jnp.cumsum(block_marks.astype(jnp.int32)) == 0).astype(jnp.float32)
        incoming = (
            jnp.einsum("ntc,nc->tc", enter_decay, residues * carry_state, precision=precise)
            * before[:, None]
        )
        tail_mask = (block_docs == block_docs[block_len - 1]).astype(jnp.float32)
        passes = 1.0 - jnp.max(block_marks.astype(jnp.float32))
        added_state = jnp.einsum(
            "nsc,s,sc->nc", leave_decay, tail_mask, block_rows, precision=precise
        )
        return (block_decay * carry_state * passes + added_state, within + incoming)

    zero_state = jnp.zeros((decay_rates.shape[0], channels), jnp.float32)
    end_state, local_out = lax.scan(
        advance,
        zero_state,
        (
            feed_in.reshape(num_blocks, block_len, channels),
            doc_index.reshape(num_blocks, block_len),
            opening.reshape(num_blocks, block_len),
        ),
    )
    local_out = local_out.reshape(length, channels)
    states_part = lax.all_gather(end_state[None], "ctx", axis=0, tiled=True)
    row_count = states_part.shape[0]
    shard_ids = jnp.arange(row_count, dtype=jnp.int32)
    shard_gap = jnp.maximum(my_shard - 1 - shard_ids, 0).astype(jnp.float32)
    in_window = ((shard_ids >= anchor) & (shard_ids < my_shard)).astype(jnp.float32)
    weight = (
        jnp.exp(-(length * shard_gap)[:, None, None] * decay_rates[None, :, :])
        * in_window[:, None, None]
    )
    carried = jnp.sum(weight * states_part, axis=0)
    offsets = jnp.arange(1, length + 1, dtype=jnp.float32)
    decay_out = jnp.exp(-offsets[None, :, None] * decay_rates[:, None, :])
    from_prior = (
        jnp.einsum("ntc,nc->tc", decay_out, residues * carried, precision=precise)
        * open_shard[:, None]
    )
    conv_total = local_out + from_prior + skip_gain[None, :] * feed_in
    hidden = (gate_out.astype(jnp.float32) * conv_total).astype(jnp.bfloat16)
    return lax.psum_scatter(
        jnp.dot(hidden, out_proj, preferred_element_type=jnp.float32).astype(jnp.bfloat16),
        "tp",
        scatter_dimension=0,
        tiled=True,
    )


def solution(mesh):
    return jax.shard_map(
        per_device,
        mesh=mesh,
        in_specs=(
            P("ctx", "tp"),
            P("ctx", "tp"),
            P("ctx", "tp"),
            P(None, "tp"),
            P(None, "tp"),
            P("tp"),
            P("tp", None),
            P(),
        ),
        out_specs=P(("ctx", "tp"), None),
        check_vma=False,
    )
```

profile of v0, /device:TPU:8, one launch (start us, length us, event | category | flops | bytes accessed | tf_op | source)
XLA Modules:
  0.0 297.7 jit_solution(3338242892878419437)
XLA Ops:
  6.5 0.7 copy.14
  7.5 1.3 fusion.11
  9.1 0.9 multiply_exponential_fusion
  10.0 1.0 multiply_reduce_fusion.5
  11.0 1.0 fusion.8
  12.3 79.1 %while.15 = (s32[]{:T(128)}, f32[16,512]{1,0:T(8,128)S(1)}, f32[16,32,512]{2,1,0:T(8,128)}, f32[16,512]{1,0:T(8,128)S(1)}, pred[16,32]{1,0:T(8,128)(4,1)S(1)}, /...) while((s32[]{:T(128)}, f32[16,512]{1,0:T(8,128)S(1)}, ...), condition=%wide.region_6.7_spmd.clone.clone.clone, body=%wide.region_3.6_spmd.clone.clone.clone.sunk | while | flops 3198147 | bytes 3157015 | solution.py:56
  13.0 0.7 compare_convert_fusion.4
  14.0 0.7 convert_reduce_fusion.5
  16.5 0.7 bitcast_dynamic-update-slice_fusion.2
  17.2 0.7 slice.12
  17.9 0.7 compare_convert_fusion.4
  19.0 0.7 convert_reduce_fusion.5
  21.5 0.7 bitcast_dynamic-update-slice_fusion.2
  22.2 0.7 slice.12
  22.8 0.7 compare_convert_fusion.4
  23.9 0.7 convert_reduce_fusion.5
  26.4 0.7 bitcast_dynamic-update-slice_fusion.2
  27.8 0.7 compare_convert_fusion.4
  28.9 0.7 convert_reduce_fusion.5
  31.4 0.7 bitcast_dynamic-update-slice_fusion.2
  32.7 0.7 compare_convert_fusion.4
  33.8 0.7 convert_reduce_fusion.5
  36.3 0.7 bitcast_dynamic-update-slice_fusion.2
  37.7 0.7 compare_convert_fusion.4
  38.8 0.7 convert_reduce_fusion.5
  41.2 0.7 bitcast_dynamic-update-slice_fusion.2
  42.0 0.7 slice.12
  42.6 0.7 compare_convert_fusion.4
  43.7 0.7 convert_reduce_fusion.5
  46.2 0.7 bitcast_dynamic-update-slice_fusion.2
  47.6 0.7 compare_convert_fusion.4
  48.6 0.7 convert_reduce_fusion.5
  51.1 0.7 bitcast_dynamic-update-slice_fusion.2
  52.5 0.7 compare_convert_fusion.4
  53.6 0.7 convert_reduce_fusion.5
  56.1 0.7 bitcast_dynamic-update-slice_fusion.2
  57.5 0.7 compare_convert_fusion.4
  58.5 0.7 convert_reduce_fusion.5
  61.0 0.7 bitcast_dynamic-update-slice_fusion.2
  62.4 0.7 compare_convert_fusion.4
  63.5 0.7 convert_reduce_fusion.5
  66.0 0.7 bitcast_dynamic-update-slice_fusion.2
  67.3 0.7 compare_convert_fusion.4
  68.4 0.7 convert_reduce_fusion.5
  70.9 0.7 bitcast_dynamic-update-slice_fusion.2
  72.3 0.7 compare_convert_fusion.4
  73.4 0.7 convert_reduce_fusion.5
  75.9 0.7 bitcast_dynamic-update-slice_fusion.2
  77.2 0.7 compare_convert_fusion.4
  78.3 0.7 convert_reduce_fusion.5
  80.8 0.7 bitcast_dynamic-update-slice_fusion.2
  81.5 0.7 slice.12
  82.2 0.7 compare_convert_fusion.4
  83.3 0.7 convert_reduce_fusion.5
  85.8 0.7 bitcast_dynamic-update-slice_fusion.2
  87.1 0.7 compare_convert_fusion.4
  88.2 0.7 convert_reduce_fusion.5
  90.7 0.7 bitcast_dynamic-update-slice_fusion.2
  96.0 140.3 %all-gather.3.cloned.1.call-done = f32[1024,512]{1,0:T(8,128)} async-done(((f32[16,512]{1,0:T(8,128)}), f32[1024,512]{1,0:T(8,128)}) %all-gather.3.cloned.1.call-update) | async-done | bytes 2097168 | tf_op jit(solution)/shard_map/all_gather | solution.py:66
  236.4 2.1 multiply_reduce_fusion.4
  238.5 2.8 multiply_reduce_fusion.3
  241.8 1.8 copy-done.10
  243.6 4.3 %convolution_convert_fusion = bf16[512,4096]{1,0:T(8,128)(2,1)} fusion(bf16[512,512]{1,0:T(8,128)(2,1)S(1)} %fusion.7, bf16[512,4096]{1,0:T(8,128)(2,1)S(1)} %copy-done.10), kind=kOutput, calls=%fused_computation.19 | convolution fusion | flops 2149580800 | bytes 8912896 | tf_op jit(solution)/shard_map/dot_general | solution.py:85
  248.0 42.9 %reduce-scatter.2.cloned.1.call-done = bf16[64,4096]{1,0:T(8,128)(2,1)} async-done(((bf16[512,4096]{1,0:T(8,128)(2,1)}), bf16[64,4096]{1,0:T(8,128)(2,1)}) %reduce-scatter.2.cloned.1.call-update) | async-done | bytes 524304 | tf_op jit(solution)/shard_map/reduce_scatter | solution.py:84
  (265 shorter events, 34.0 us)
Async XLA Ops:
  6.5 229.8 %all-gather.3.cloned.1.call-start = ((), (), s32[]{:S(2)}) async-start(), calls=%async_computation.2 | async-start | bytes 2129920 | tf_op jit(solution)/shard_map/all_gather | solution.py:66
  9.1 2.9 copy-start
  9.1 3.0 copy-start.2
  11.0 1.2 copy-start.4
  11.0 1.2 copy-start.8
  91.4 0.6 copy-start.5
  92.0 198.8 %reduce-scatter.2.cloned.1.call-start = ((), (), s32[]{:S(2)}) async-start(), calls=%async_computation.1 | async-start | bytes 4718592 | tf_op jit(solution)/shard_map/reduce_scatter | solution.py:84
  238.5 2.9 copy-start.1
  238.5 2.9 copy-start.3
  238.5 2.9 copy-start.6
  238.5 2.9 copy-start.7
  238.5 2.9 copy-start.9
  241.4 2.2 copy-start.10
Sparse Core Ops, SparseCore 0:
  92.2 144.1 all-gather.2
  248.1 42.7 reduce-scatter.1
where the time goes:
time: 298 us
  waiting for transfers between devices  183 us (61%)
  other arithmetic  64.3 us (22%)
  between operations  16.4 us (6%)
  local copies, waits for them, and re-layouts  16.3 us (5%)
  loops' own time  12 us (4%)
  matrix products  5.35 us (2%)
    all_gather x1, waiting for transfers between devices, per_device(): states_part = lax.all_gather(end_state[None], 'ctx', axis=0, tiled=True)  140 us
    reduce_scatter x1, waiting for transfers between devices, per_device(): lax.psum_scatter(jnp.dot(hidden, out_proj, preferred_element_type=jnp.flo...  42.9 us
    another operation x34, other arithmetic  12.2 us
    another operation x1, loops' own time, per_device(): lax.scan(advance, zero_state, (feed_in.reshape(num_blocks, block_len, cha...  12 us
    dynamic_update_slice x16, other arithmetic, per_device(): lax.scan(advance, zero_state, (feed_in.reshape(num_blocks, block_len, cha...  11.2 us
    reduce_max x16, other arithmetic, advance(): passes = 1.0 - jnp.max(block_marks.astype(jnp.float32))  11.1 us
    slice x16, local copies, waits for them, and re-layouts, advance(): tail_mask = (block_docs == block_docs[block_len - 1]).astype(jnp.float32)  10.6 us
    dot_general x16, other arithmetic, advance(): jnp.einsum('tsc,sc->tc', toeplitz * same_doc[:, :, None], block_rows, pre...  7.12 us
  transfers between devices with their start and end apart: 2, of which 2 were waited for; matrix products, arithmetic and copies ran while one was open for 0% of the time, Pallas kernels for 0%

commit v1 on v0

--- a/solution.py
+++ b/solution.py
@@ -63,7 +63,9 @@
         ),
     )
     local_out = local_out.reshape(length, channels)
-    states_part = lax.all_gather(end_state[None], "ctx", axis=0, tiled=True)
+    states_part = jnp.concatenate(
+        lax.all_to_all(jnp.stack([end_state[None]] * lax.axis_size("ctx")), "ctx", 0, 0), axis=0
+    )
     row_count = states_part.shape[0]
     shard_ids = jnp.arange(row_count, dtype=jnp.int32)
     shard_gap = jnp.maximum(my_shard - 1 - shard_ids, 0).astype(jnp.float32)

time: 298 us -> 266 us (0.89)
  waiting for transfers between devices: 183 us -> 133 us
  starting transfers between devices: 0.04 us -> 18.8 us
    all_gather x1 -> x0, waiting for transfers between devices: 140 us -> none  [per_device(): states_part = lax.all_gather(end_state[None], 'ctx', axis=0, tiled=True)]
    all_to_all x0 -> x1, waiting for transfers between devices: none -> 93.5 us  [per_device(): lax.all_to_all(jnp.stack([end_state[None]] * lax.axis_size('ctx')), 'ctx'...]
    all_to_all x0 -> x1, starting transfers between devices: none -> 18.7 us  [per_device(): lax.all_to_all(jnp.stack([end_state[None]] * lax.axis_size('ctx')), 'ctx'...]
    reduce_scatter x1, waiting for transfers between devices: 42.9 us -> 39.5 us  [per_device(): lax.psum_scatter(jnp.dot(hidden, out_proj, preferred_element_type=jnp.flo...]
where the time goes in v1:
time: 266 us
  waiting for transfers between devices  133 us (50%)
  other arithmetic  62.8 us (24%)
  starting transfers between devices  18.8 us (7%)
  local copies, waits for them, and re-layouts  17.3 us (7%)
  between operations  16.4 us (6%)
  loops' own time  12 us (5%)
  matrix products  5.36 us (2%)
    all_to_all x1, waiting for transfers between devices, per_device(): lax.all_to_all(jnp.stack([end_state[None]] * lax.axis_size('ctx')), 'ctx'...  93.5 us
    reduce_scatter x1, waiting for transfers between devices, per_device(): lax.psum_scatter(jnp.dot(hidden, out_proj, preferred_element_type=jnp.flo...  39.5 us
    all_to_all x1, starting transfers between devices, per_device(): lax.all_to_all(jnp.stack([end_state[None]] * lax.axis_size('ctx')), 'ctx'...  18.7 us
    another operation x34, other arithmetic  12.2 us
    another operation x1, loops' own time, per_device(): lax.scan(advance, zero_state, (feed_in.reshape(num_blocks, block_len, cha...  12 us
    dynamic_update_slice x16, other arithmetic, per_device(): lax.scan(advance, zero_state, (feed_in.reshape(num_blocks, block_len, cha...  11.2 us
    reduce_max x16, other arithmetic, advance(): passes = 1.0 - jnp.max(block_marks.astype(jnp.float32))  11.1 us
    slice x16, local copies, waits for them, and re-layouts, advance(): tail_mask = (block_docs == block_docs[block_len - 1]).astype(jnp.float32)  10.6 us
  transfers between devices with their start and end apart: 2, of which 2 were waited for; matrix products, arithmetic and copies ran while one was open for 0% of the time, Pallas kernels for 0%

profile of v1, /device:TPU:8, one launch (start us, length us, event | category | flops | bytes accessed | tf_op | source)
XLA Modules:
  0.0 265.6 jit_solution(12416678031092720459)
XLA Ops:
  6.5 0.7 copy.16
  7.5 1.3 fusion.12
  9.1 0.9 multiply_exponential_fusion
  10.0 1.0 multiply_reduce_fusion.4
  11.0 1.0 fusion.9
  12.3 79.1 %while.15 = (s32[]{:T(128)}, f32[16,512]{1,0:T(8,128)S(1)}, f32[16,32,512]{2,1,0:T(8,128)}, f32[16,512]{1,0:T(8,128)S(1)}, pred[16,32]{1,0:T(8,128)(4,1)S(1)}, /...) while((s32[]{:T(128)}, f32[16,512]{1,0:T(8,128)S(1)}, ...), condition=%wide.region_6.7_spmd.clone.clone.clone, body=%wide.region_3.6_spmd.clone.clone.clone.sunk | while | flops 3198147 | bytes 3157015 | solution.py:56
  13.0 0.7 compare_convert_fusion.4
  14.0 0.7 convert_reduce_fusion.5
  16.5 0.7 bitcast_dynamic-update-slice_fusion.2
  17.2 0.7 slice.12
  17.9 0.7 compare_convert_fusion.4
  19.0 0.7 convert_reduce_fusion.5
  21.5 0.7 bitcast_dynamic-update-slice_fusion.2
  22.8 0.7 compare_convert_fusion.4
  23.9 0.7 convert_reduce_fusion.5
  26.4 0.7 bitcast_dynamic-update-slice_fusion.2
  27.8 0.7 compare_convert_fusion.4
  28.9 0.7 convert_reduce_fusion.5
  31.4 0.7 bitcast_dynamic-update-slice_fusion.2
  32.1 0.7 slice.12
  32.7 0.7 compare_convert_fusion.4
  33.8 0.7 convert_reduce_fusion.5
  36.3 0.7 bitcast_dynamic-update-slice_fusion.2
  37.7 0.7 compare_convert_fusion.4
  38.8 0.7 convert_reduce_fusion.5
  41.2 0.7 bitcast_dynamic-update-slice_fusion.2
  42.6 0.7 compare_convert_fusion.4
  43.7 0.7 convert_reduce_fusion.5
  46.2 0.7 bitcast_dynamic-update-slice_fusion.2
  47.6 0.7 compare_convert_fusion.4
  48.6 0.7 convert_reduce_fusion.5
  51.1 0.7 bitcast_dynamic-update-slice_fusion.2
  51.8 0.7 slice.12
  52.5 0.7 compare_convert_fusion.4
  53.6 0.7 convert_reduce_fusion.5
  56.1 0.7 bitcast_dynamic-update-slice_fusion.2
  57.5 0.7 compare_convert_fusion.4
  58.5 0.7 convert_reduce_fusion.5
  61.0 0.7 bitcast_dynamic-update-slice_fusion.2
  62.4 0.7 compare_convert_fusion.4
  63.5 0.7 convert_reduce_fusion.5
  66.0 0.7 bitcast_dynamic-update-slice_fusion.2
  67.3 0.7 compare_convert_fusion.4
  68.4 0.7 convert_reduce_fusion.5
  70.9 0.7 bitcast_dynamic-update-slice_fusion.2
  72.3 0.7 compare_convert_fusion.4
  73.4 0.7 convert_reduce_fusion.5
  75.9 0.7 bitcast_dynamic-update-slice_fusion.2
  77.2 0.7 compare_convert_fusion.4
  78.3 0.7 convert_reduce_fusion.5
  80.8 0.7 bitcast_dynamic-update-slice_fusion.2
  82.2 0.7 compare_convert_fusion.4
  83.3 0.7 convert_reduce_fusion.5
  85.8 0.7 bitcast_dynamic-update-slice_fusion.2
  87.1 0.7 compare_convert_fusion.4
  88.2 0.7 convert_reduce_fusion.5
  90.7 0.7 bitcast_dynamic-update-slice_fusion.2
  91.4 1.6 stack.3
  93.0 18.7 %all-to-all-start = ((f32[64,1,16,512]{3,2,1,0:T(8,128)}), f32[64,1,16,512]{3,2,1,0:T(8,128)S(1)}, u32[]{:S(2)}, u32[]{:S(2)}) async-start(f32[64,1,16,512]{3,2,1,0:T(8,128)} %stack.3), calls=%async_computation | async-start | bytes 4194304 | tf_op jit(solution)/shard_map/all_to_all | solution.py:67
  115.8 93.5 %all-to-all-done = f32[64,1,16,512]{3,2,1,0:T(8,128)S(1)} async-done(((f32[64,1,16,512]{3,2,1,0:T(8,128)}), f32[64,1,16,512]{3,2,1,0:T(8,128)S(1)}, u32[]{:S(2)}, u32[]{:S(2)}) %all-to-all-start) | async-done | bytes 2097184 | tf_op jit(solution)/shard_map/all_to_all | solution.py:67
  209.8 2.8 %multiply_reduce_fusion.3 = f32[512,512]{0,1:T(8,128)S(1)} fusion(f32[512,16]{0,1:T(8,128)S(1)} %multiply_bitcast_fusion.1, f32[16,512]{1,0:T(8,128)S(1)} %get-tuple-element.333, f32[512]{0:T(512)S(1)} %add_negate_fusion), kind=kLoop, calls=%fused_computation.18 | loop fusion | flops 12320768 | bytes 1116160 | tf_op jit(solution)/shard_map/ntc,nc->tc/dot_general | solution.py:81
  213.1 1.8 copy-done.9
  214.9 4.3 %convolution_convert_fusion = bf16[512,4096]{1,0:T(8,128)(2,1)} fusion(bf16[512,512]{1,0:T(8,128)(2,1)S(1)} %fusion.8, bf16[512,4096]{1,0:T(8,128)(2,1)S(1)} %copy-done.9), kind=kOutput, calls=%fused_computation.19 | convolution fusion | flops 2149580800 | bytes 8912896 | tf_op jit(solution)/shard_map/dot_general | solution.py:87
  219.3 39.5 %reduce-scatter.2.cloned.1.call-done = bf16[64,4096]{1,0:T(8,128)(2,1)} async-done(((bf16[512,4096]{1,0:T(8,128)(2,1)}), bf16[64,4096]{1,0:T(8,128)(2,1)}) %reduce-scatter.2.cloned.1.call-update) | async-done | bytes 524304 | tf_op jit(solution)/shard_map/reduce_scatter | solution.py:86
  (263 shorter events, 34.5 us)
Async XLA Ops:
  9.1 3.0 %copy-start = (bf16[512,512]{1,0:T(8,128)(2,1)S(1)}, bf16[512,512]{1,0:T(8,128)(2,1)}, u32[]{:S(2)}) copy-start(bf16[512,512]{1,0:T(8,128)(2,1)} %param.12) | copy-start | bytes 1572868
  9.1 3.0 %copy-start.2 = (bf16[512,512]{1,0:T(8,128)(2,1)S(1)}, bf16[512,512]{1,0:T(8,128)(2,1)}, u32[]{:S(2)}) copy-start(bf16[512,512]{1,0:T(8,128)(2,1)} %param.11) | copy-start | bytes 1572868
  11.0 1.2 copy-start.4
  11.0 1.2 copy-start.7
  93.0 116.2 %all-to-all-start = ((f32[64,1,16,512]{3,2,1,0:T(8,128)}), f32[64,1,16,512]{3,2,1,0:T(8,128)S(1)}, u32[]{:S(2)}, u32[]{:S(2)}) async-start(f32[64,1,16,512]{3,2,1,0:T(8,128)} %stack.3), calls=%async_computation | async-start | bytes 4194304 | tf_op jit(solution)/shard_map/all_to_all | solution.py:67
  111.8 147.0 %reduce-scatter.2.cloned.1.call-start = ((), (), s32[]{:S(2)}) async-start(), calls=%async_computation.2 | async-start | bytes 4718592 | tf_op jit(solution)/shard_map/reduce_scatter | solution.py:86
  209.8 2.9 %copy-start.1 = (bf16[512,512]{1,0:T(8,128)(2,1)S(1)}, bf16[512,512]{1,0:T(8,128)(2,1)}, u32[]{:S(2)}) copy-start(bf16[512,512]{1,0:T(8,128)(2,1)} %param.12) | copy-start | bytes 1572868
  209.8 2.9 %copy-start.3 = (bf16[512,512]{1,0:T(8,128)(2,1)S(1)}, bf16[512,512]{1,0:T(8,128)(2,1)}, u32[]{:S(2)}) copy-start(bf16[512,512]{1,0:T(8,128)(2,1)} %param.11) | copy-start | bytes 1572868
  209.8 2.9 %copy-start.5 = (f32[16,32,512]{2,1,0:T(8,128)S(1)}, f32[16,32,512]{2,1,0:T(8,128)}, u32[]{:S(2)}) copy-start(f32[16,32,512]{2,1,0:T(8,128)} %get-tuple-element.63) | copy-start | bytes 3145732
  209.8 2.9 %copy-start.6 = (bf16[512,512]{1,0:T(8,128)(2,1)S(1)}, bf16[512,512]{1,0:T(8,128)(2,1)}, u32[]{:S(2)}) copy-start(bf16[512,512]{1,0:T(8,128)(2,1)} %param.10) | copy-start | bytes 1572868
  209.8 2.9 %copy-start.8 = (f32[512]{0:T(512)S(1)}, f32[512]{0:T(512)}, u32[]{:S(2)}) copy-start(f32[512]{0:T(512)} %param.15) | copy-start | bytes 6148
  212.7 2.2 copy-start.9
Sparse Core Ops, SparseCore 0:
  219.4 39.3 reduce-scatter.1
